TPU v7x, 256 devices: a whole 4x4x8 slice. The times are simulated.
256 devices in a mesh: cfg: 2 (over core), req: 16 (over x_hi, z), seq: 8 (over x_lo, y).
Axes of the slice: x: 4 (x_hi: 2, x_lo: 2; x = x_hi * 2 + x_lo), y: 4, z: 8, core: 2. Of those that a mesh axis runs over, the one named last changes fastest.
Arguments:
- hidden: bfloat16 [2, 16, 2304, 1536], P('cfg', 'req', 'seq'), may hold values from -6 to 6
- latent: float32 [16, 2304, 64], P('req', 'seq', 'cfg'), may hold values from -6 to 6
- modulation: float32 [16, 5, 1536], P('req'), may hold values from -3 to 3
- w_qkv: bfloat16 [1536, 4608], P('req'), may hold values from -1 to 1
- w_out: bfloat16 [1536, 1536], P('req'), may hold values from -0.15625 to 0.15625
- q_gain: float32 [1536], replicated, may hold values from 0 to 2
- k_gain: float32 [1536], replicated, may hold values from 0 to 2
- w_head: bfloat16 [1536, 64], replicated, may hold values from -0.15625 to 0.15625
- lengths: int32 [16], P('req'), may hold values from 288 to 2304, as said below
- guidance: float32 [16], P('req'), may hold values from 3 to 7
- step_size: float32 [16], P('req'), may hold values from 0.03 to 0.3
Outputs:
- new_latent: float32 [16, 2304, 64], P('req', 'seq', 'cfg')
Inputs may be any that keep to these rules, and one draw needn't show every extreme that they name: `lengths`: some request has exactly 2304 video tokens in every draw.
All inputs are finite; a program needn't handle non-finite values.
Results may differ from a plain program's by a relative error of at most 0.01.
Values may be sent and summed in bfloat16 or wider, within the bound.
A program may use at most 128 MiB of HBM per device.

v0:
```python
import jax
import jax.numpy as jnp
from jax import lax
from jax.sharding import PartitionSpec as P

DH = 128


def passed_along(value, axis, steps):
    count = lax.axis_size(axis)
    pairs = [(source, (source + steps) % count) for source in range(count)]
    return lax.ppermute(value, axis, pairs)


def from_partner(value, axis, apart):
    mask = 2**apart
    pairs = [(source, source ^ mask) for source in range(lax.axis_size(axis))]
    return lax.ppermute(value, axis, pairs)


def layer_norm(values):
    centered = values - jnp.mean(values, axis=-1, keepdims=True)
    return centered / jnp.sqrt(jnp.mean(centered * centered, axis=-1, keepdims=True) + 1e-06)


def rms_gain(values, gain):
    return values / jnp.sqrt(jnp.mean(values * values, axis=-1, keepdims=True) + 1e-06) * gain


def add_rows(left, piece):
    return jnp.dot(left, piece, preferred_element_type=jnp.float32)


def attend(state, query, stacked, start, length):
    top, total, weighted = state
    keys = stacked[0]
    values = stacked[1]
    count = keys.shape[0]
    scores = jnp.einsum("qhd,khd->qhk", query, keys, preferred_element_type=jnp.float32) / jnp.sqrt(
        jnp.float32(query.shape[2])
    )
    valid = start + jnp.arange(count, dtype=jnp.int32) < length
    scores = jnp.where(valid[None, None, :], scores, jnp.float32(-1e30))
    new_top = jnp.maximum(top, jnp.max(scores, axis=-1))
    factor = jnp.exp(top - new_top)
    probs = jnp.where(valid[None, None, :], jnp.exp(scores - new_top[:, :, None]), jnp.float32(0.0))
    total = total * factor + jnp.sum(probs, axis=-1)
    weighted = weighted * factor[:, :, None] + jnp.einsum(
        "qhk,khd->qhd", probs.astype(jnp.bfloat16), values, preferred_element_type=jnp.float32
    )
    return (new_top, total, weighted)


def local(
    hidden, latent, modulation, w_qkv, w_out, q_gain, k_gain, w_head, lengths, guidance, step_size
):
    state = hidden[0, 0]
    modes = modulation[0]
    length = lengths[0]
    rows = state.shape[0]
    width = state.shape[1]
    heads = q_gain.shape[0] // DH
    wide = state.astype(jnp.float32)
    normed = (layer_norm(wide) * (1.0 + modes[1]) + modes[0]).astype(jnp.bfloat16)
    qkv = add_rows(normed, lax.all_gather(w_qkv, "req", axis=0, tiled=True))
    query = rms_gain(qkv[:, :width], q_gain).astype(jnp.bfloat16).reshape(rows, heads, DH)
    keys = rms_gain(qkv[:, width : 2 * width], k_gain).astype(jnp.bfloat16).reshape(rows, heads, DH)
    values = qkv[:, 2 * width :].astype(jnp.bfloat16).reshape(rows, heads, DH)
    stacked = jnp.stack([keys, values])
    position = lax.axis_index("seq")
    members = lax.axis_size("seq")
    start_state = (
        jnp.full((rows, heads), -1e30, jnp.float32),
        jnp.zeros((rows, heads), jnp.float32),
        jnp.zeros((rows, heads, DH), jnp.float32),
    )
    first = attend(start_state, query, stacked, position * rows, length)

    def cycle_step(turn, carry):
        moving, inner = carry
        moving = passed_along(moving, "seq", 1)
        source = (position - turn) % members
        return (moving, attend(inner, query, moving, source * rows, length))

    moved, result = lax.fori_loop(1, members, cycle_step, (stacked, first))
    top, total, weighted = result
    attended = (weighted / total[:, :, None]).reshape(rows, width).astype(jnp.bfloat16)
    projected = add_rows(attended, lax.all_gather(w_out, "req", axis=0, tiled=True))
    block_out = (wide + modes[2] * projected).astype(jnp.bfloat16)
    head_in = (layer_norm(block_out.astype(jnp.float32)) * (1.0 + modes[4]) + modes[3]).astype(
        jnp.bfloat16
    )
    velocity = jnp.dot(head_in, w_head, preferred_element_type=jnp.float32)
    branch = lax.axis_index("cfg")
    scale = guidance[0]
    channels = velocity.shape[1] // 2
    own = lax.dynamic_slice_in_dim(velocity, branch * channels, channels, 1)
    outgoing = lax.dynamic_slice_in_dim(velocity, (1 - branch) * channels, channels, 1)
    other = from_partner(outgoing.astype(jnp.bfloat16), "cfg", 0).astype(outgoing.dtype)
    cond = jnp.where(branch == 0, own, other)
    uncond = jnp.where(branch == 0, other, own)
    guided = uncond + scale * (cond - uncond)
    valid = position * rows + jnp.arange(rows, dtype=jnp.int32) < length
    current = latent[0]
    updated = jnp.where(valid[:, None], current - step_size[0] * guided, current)
    return updated[None]


def solution(mesh):
    return jax.shard_map(
        local,
        mesh=mesh,
        in_specs=(
            P("cfg", "req", "seq", None),
            P("req", "seq", "cfg"),
            P("req", None, None),
            P("req", None),
            P("req", None),
            P(),
            P(),
            P(),
            P("req"),
            P("req"),
            P("req"),
        ),
        out_specs=P("req", "seq", "cfg"),
        check_vma=False,
    )
```

profile of v0, /device:TPU:1, one launch (start us, length us, event | category | flops | bytes accessed | tf_op | source)
XLA Modules:
  0.0 648.4 jit_solution(9502393456810084686)
XLA Ops:
  10.2 198.2 %all-gather.3.cloned.1.call-done = bf16[1536,4608]{1,0:T(8,128)(2,1)} async-done(((bf16[96,4608]{1,0:T(8,128)(2,1)}), bf16[1536,4608]{1,0:T(8,128)(2,1)}) %all-gather.3.cloned.1.call-update) | async-done | bytes 14155792 | tf_op jit(solution)/shard_map/all_gather | solution.py:65
  208.3 7.9 %fusion.42 = f32[288,4608]{1,0:T(8,128)S(1)} fusion(bf16[1536,4608]{1,0:T(8,128)(2,1)} %all-gather.3.cloned.1.call-done, bf16[1,1,288,1536]{3,2,1,0:T(8,128)(2,1)S(1)} %copy-done.2, f32[1536]{0:T(1024)S(1)} %get-tuple-element.226, f32[1536]{0:T(1024)S(1)} %get-tuple-element.227, f32[288]{0:T(512)S(1)} %add_sqrt_fusion.3, f32[288]{0:T(512)S(1)} %broadcast_multiply_fusion.1), kind=kOutput, calls=%fused_computation.61 | convolution fusion | flops 4079517696 | bytes 20363520 | tf_op jit(solution)/shard_map/dot_general | solution.py:31
  216.7 1.9 copy-done.1
  218.6 1.5 fusion.56
  220.1 1.0 copy-done.4
  222.8 1.7 copy.25
  224.7 1.0 copy-done.5
  225.7 1.0 bitcast_reduce_fusion.1
  226.7 1.5 fusion.21
  228.2 5.1 bitcast_add_fusion.1
  233.3 75.5 %all-gather.5.cloned.1.call-done = bf16[1536,1536]{1,0:T(8,128)(2,1)} async-done(((bf16[96,1536]{1,0:T(8,128)(2,1)}), bf16[1536,1536]{1,0:T(8,128)(2,1)}) %all-gather.5.cloned.1.call-update) | async-done | bytes 4718608 | tf_op jit(solution)/shard_map/all_gather | solution.py:88
  308.7 315.1 %while.21 = (s32[]{:T(128)}, bf16[2,288,12,128]{3,1,2,0:T(8,128)(2,1)}, f32[288,12]{0,1:T(8,128)S(1)}, f32[288,12]{0,1:T(8,128)S(1)}, f32[288,12,128]{2,0,1:T(8,...) while((s32[]{:T(128)}, ...), condition=%wide.region_9.10_spmd, body=%wide.region_6.9_spmd.sunk | while | flops 523439424 | bytes 44481960 | solution.py:85
  308.7 1.2 collective-permute-start
  310.6 36.8 %collective-permute-done = bf16[2,288,12,128]{3,1,2,0:T(8,128)(2,1)S(1)} collective-permute-done((bf16[2,288,12,128]{3,1,2,0:T(8,128)(2,1)}, bf16[2,288,12,128]{3,1,2,0:T(8,128)(2,1)S(1)}, u32[]{:S(2)}, u32[]{:S(2)}) %collective-permute-start) | collective-permute-done | bytes 1769504 | tf_op jit(solution)/shard_map/while/body/eval_jaxpr/ppermute | solution.py:12
  347.3 0.9 bitcast_reduce_fusion.3
  348.3 1.5 fusion.80
  349.8 1.3 copy.66
  351.1 0.8 copy-done.9
  351.9 3.1 bitcast_add_fusion.3
  355.0 1.3 copy-done.10
  357.0 37.1 %collective-permute-done = bf16[2,288,12,128]{3,1,2,0:T(8,128)(2,1)S(1)} collective-permute-done((bf16[2,288,12,128]{3,1,2,0:T(8,128)(2,1)}, bf16[2,288,12,128]{3,1,2,0:T(8,128)(2,1)S(1)}, u32[]{:S(2)}, u32[]{:S(2)}) %collective-permute-start) | collective-permute-done | bytes 1769504 | tf_op jit(solution)/shard_map/while/body/eval_jaxpr/ppermute | solution.py:12
  394.1 0.9 bitcast_reduce_fusion.3
  395.1 1.5 fusion.80
  396.6 1.3 copy.66
  397.8 0.8 copy-done.9
  398.7 3.1 bitcast_add_fusion.3
  401.8 1.3 copy-done.10
  403.7 36.3 %collective-permute-done = bf16[2,288,12,128]{3,1,2,0:T(8,128)(2,1)S(1)} collective-permute-done((bf16[2,288,12,128]{3,1,2,0:T(8,128)(2,1)}, bf16[2,288,12,128]{3,1,2,0:T(8,128)(2,1)S(1)}, u32[]{:S(2)}, u32[]{:S(2)}) %collective-permute-start) | collective-permute-done | bytes 1769504 | tf_op jit(solution)/shard_map/while/body/eval_jaxpr/ppermute | solution.py:12
  440.0 0.9 bitcast_reduce_fusion.3
  440.9 1.5 fusion.80
  442.4 1.3 copy.66
  443.7 0.8 copy-done.9
  444.6 3.1 bitcast_add_fusion.3
  447.6 1.3 copy-done.10
  449.6 35.4 %collective-permute-done = bf16[2,288,12,128]{3,1,2,0:T(8,128)(2,1)S(1)} collective-permute-done((bf16[2,288,12,128]{3,1,2,0:T(8,128)(2,1)}, bf16[2,288,12,128]{3,1,2,0:T(8,128)(2,1)S(1)}, u32[]{:S(2)}, u32[]{:S(2)}) %collective-permute-start) | collective-permute-done | bytes 1769504 | tf_op jit(solution)/shard_map/while/body/eval_jaxpr/ppermute | solution.py:12
  485.0 0.9 bitcast_reduce_fusion.3
  485.9 1.5 fusion.80
  487.5 1.3 copy.66
  488.7 0.8 copy-done.9
  489.6 3.1 bitcast_add_fusion.3
  492.6 1.3 copy-done.10
  494.6 34.5 %collective-permute-done = bf16[2,288,12,128]{3,1,2,0:T(8,128)(2,1)S(1)} collective-permute-done((bf16[2,288,12,128]{3,1,2,0:T(8,128)(2,1)}, bf16[2,288,12,128]{3,1,2,0:T(8,128)(2,1)S(1)}, u32[]{:S(2)}, u32[]{:S(2)}) %collective-permute-start) | collective-permute-done | bytes 1769504 | tf_op jit(solution)/shard_map/while/body/eval_jaxpr/ppermute | solution.py:12
  529.1 0.9 bitcast_reduce_fusion.3
  530.1 1.5 fusion.80
  531.6 1.3 copy.66
  532.9 0.8 copy-done.9
  533.7 3.1 bitcast_add_fusion.3
  536.8 1.3 copy-done.10
  538.8 33.7 %collective-permute-done = bf16[2,288,12,128]{3,1,2,0:T(8,128)(2,1)S(1)} collective-permute-done((bf16[2,288,12,128]{3,1,2,0:T(8,128)(2,1)}, bf16[2,288,12,128]{3,1,2,0:T(8,128)(2,1)S(1)}, u32[]{:S(2)}, u32[]{:S(2)}) %collective-permute-start) | collective-permute-done | bytes 1769504 | tf_op jit(solution)/shard_map/while/body/eval_jaxpr/ppermute | solution.py:12
  572.4 0.9 bitcast_reduce_fusion.3
  573.4 1.5 fusion.80
  574.9 1.3 copy.66
  576.2 0.8 copy-done.9
  577.0 3.1 bitcast_add_fusion.3
  580.1 1.3 copy-done.10
  582.1 32.8 %collective-permute-done = bf16[2,288,12,128]{3,1,2,0:T(8,128)(2,1)S(1)} collective-permute-done((bf16[2,288,12,128]{3,1,2,0:T(8,128)(2,1)}, bf16[2,288,12,128]{3,1,2,0:T(8,128)(2,1)S(1)}, u32[]{:S(2)}, u32[]{:S(2)}) %collective-permute-start) | collective-permute-done | bytes 1769504 | tf_op jit(solution)/shard_map/while/body/eval_jaxpr/ppermute | solution.py:12
  614.9 0.9 bitcast_reduce_fusion.3
  615.9 1.5 fusion.80
  617.4 1.3 copy.66
  618.6 0.8 copy-done.9
  619.5 3.1 bitcast_add_fusion.3
  622.6 1.3 copy-done.10
  623.8 4.8 fusion.67
  629.6 9.9 %collective-permute-start.1 = (bf16[288,32]{0,1:T(8,128)(2,1)S(1)}, bf16[288,32]{0,1:T(8,128)(2,1)S(1)}, u32[]{:S(2)}, u32[]{:S(2)}) collective-permute-start(bf16[288,32]{0,1:T(8,128)(2,1)S(1)} %dynamic-slice_convert_fusion), channel_id=1, source_target_pairs={{0,128},{128,0},{1,129},{129,1},{2,130},{130,2},{3,131},{131,3},{4... | collective-permute-start | bytes 55304 | tf_op jit(solution)/shard_map/ppermute | solution.py:18
  (89 shorter events, 11.5 us)
Async XLA Ops:
  6.5 622.5 %copy-start = (bf16[1536,64]{0,1:T(8,128)(2,1)S(1)}, bf16[1536,64]{0,1:T(8,128)(2,1)}, u32[]{:S(2)}) copy-start(bf16[1536,64]{0,1:T(8,128)(2,1)} %param.20) | copy-start | bytes 589828
  6.5 3.0 copy-start.2
  6.5 201.8 %all-gather.3.cloned.1.call-start = ((), (), s32[]{:S(2)}) async-start(), calls=%async_computation | async-start | bytes 15040512 | tf_op jit(solution)/shard_map/all_gather | solution.py:65
  7.3 301.5 %all-gather.5.cloned.1.call-start = ((), (), s32[]{:S(2)}) async-start(), calls=%async_computation.1 | async-start | bytes 5013504 | tf_op jit(solution)/shard_map/all_gather | solution.py:88
  216.2 2.3 copy-start.1
  216.4 2.2 copy-start.7
  216.4 2.2 copy-start.8
  220.1 1.0 copy-start.4
  222.8 1.7 copy-start.3
  224.5 1.2 copy-start.5
  308.7 38.6 %collective-permute-start = (bf16[2,288,12,128]{3,1,2,0:T(8,128)(2,1)}, bf16[2,288,12,128]{3,1,2,0:T(8,128)(2,1)S(1)}, u32[]{:S(2)}, u32[]{:S(2)}) collective-permute-start(bf16[2,288,12,128]{3,1,2,0:T(8,128)(2,1)} %get-tuple-element.331), channel_id=1, source_target_pairs={{0,1},{1,2},{2,3},{3,4},{4,5},{5,6},{6,7},{7,0},{8,9},{9,10},{10,1... | collective-permute-start | bytes 5308424 | tf_op jit(solution)/shard_map/while/body/eval_jaxpr/ppermute | solution.py:12
  349.8 2.1 copy-start.9
  355.0 1.3 copy-start.10
  356.3 37.8 %collective-permute-start = (bf16[2,288,12,128]{3,1,2,0:T(8,128)(2,1)}, bf16[2,288,12,128]{3,1,2,0:T(8,128)(2,1)S(1)}, u32[]{:S(2)}, u32[]{:S(2)}) collective-permute-start(bf16[2,288,12,128]{3,1,2,0:T(8,128)(2,1)} %get-tuple-element.331), channel_id=1, source_target_pairs={{0,1},{1,2},{2,3},{3,4},{4,5},{5,6},{6,7},{7,0},{8,9},{9,10},{10,1... | collective-permute-start | bytes 5308424 | tf_op jit(solution)/shard_map/while/body/eval_jaxpr/ppermute | solution.py:12
  396.6 2.1 copy-start.9
  401.8 1.3 copy-start.10
  403.0 36.9 %collective-permute-start = (bf16[2,288,12,128]{3,1,2,0:T(8,128)(2,1)}, bf16[2,288,12,128]{3,1,2,0:T(8,128)(2,1)S(1)}, u32[]{:S(2)}, u32[]{:S(2)}) collective-permute-start(bf16[2,288,12,128]{3,1,2,0:T(8,128)(2,1)} %get-tuple-element.331), channel_id=1, source_target_pairs={{0,1},{1,2},{2,3},{3,4},{4,5},{5,6},{6,7},{7,0},{8,9},{9,10},{10,1... | collective-permute-start | bytes 5308424 | tf_op jit(solution)/shard_map/while/body/eval_jaxpr/ppermute | solution.py:12
  442.4 2.1 copy-start.9
  447.6 1.3 copy-start.10
  448.9 36.0 %collective-permute-start = (bf16[2,288,12,128]{3,1,2,0:T(8,128)(2,1)}, bf16[2,288,12,128]{3,1,2,0:T(8,128)(2,1)S(1)}, u32[]{:S(2)}, u32[]{:S(2)}) collective-permute-start(bf16[2,288,12,128]{3,1,2,0:T(8,128)(2,1)} %get-tuple-element.331), channel_id=1, source_target_pairs={{0,1},{1,2},{2,3},{3,4},{4,5},{5,6},{6,7},{7,0},{8,9},{9,10},{10,1... | collective-permute-start | bytes 5308424 | tf_op jit(solution)/shard_map/while/body/eval_jaxpr/ppermute | solution.py:12
  487.5 2.1 copy-start.9
  492.6 1.3 copy-start.10
  493.9 35.2 %collective-permute-start = (bf16[2,288,12,128]{3,1,2,0:T(8,128)(2,1)}, bf16[2,288,12,128]{3,1,2,0:T(8,128)(2,1)S(1)}, u32[]{:S(2)}, u32[]{:S(2)}) collective-permute-start(bf16[2,288,12,128]{3,1,2,0:T(8,128)(2,1)} %get-tuple-element.331), channel_id=1, source_target_pairs={{0,1},{1,2},{2,3},{3,4},{4,5},{5,6},{6,7},{7,0},{8,9},{9,10},{10,1... | collective-permute-start | bytes 5308424 | tf_op jit(solution)/shard_map/while/body/eval_jaxpr/ppermute | solution.py:12
  531.6 2.1 copy-start.9
  536.8 1.3 copy-start.10
  538.1 34.3 %collective-permute-start = (bf16[2,288,12,128]{3,1,2,0:T(8,128)(2,1)}, bf16[2,288,12,128]{3,1,2,0:T(8,128)(2,1)S(1)}, u32[]{:S(2)}, u32[]{:S(2)}) collective-permute-start(bf16[2,288,12,128]{3,1,2,0:T(8,128)(2,1)} %get-tuple-element.331), channel_id=1, source_target_pairs={{0,1},{1,2},{2,3},{3,4},{4,5},{5,6},{6,7},{7,0},{8,9},{9,10},{10,1... | collective-permute-start | bytes 5308424 | tf_op jit(solution)/shard_map/while/body/eval_jaxpr/ppermute | solution.py:12
  574.9 2.1 copy-start.9
  580.1 1.3 copy-start.10
  581.4 33.5 %collective-permute-start = (bf16[2,288,12,128]{3,1,2,0:T(8,128)(2,1)}, bf16[2,288,12,128]{3,1,2,0:T(8,128)(2,1)S(1)}, u32[]{:S(2)}, u32[]{:S(2)}) collective-permute-start(bf16[2,288,12,128]{3,1,2,0:T(8,128)(2,1)} %get-tuple-element.331), channel_id=1, source_target_pairs={{0,1},{1,2},{2,3},{3,4},{4,5},{5,6},{6,7},{7,0},{8,9},{9,10},{10,1... | collective-permute-start | bytes 5308424 | tf_op jit(solution)/shard_map/while/body/eval_jaxpr/ppermute | solution.py:12
  617.4 2.1 copy-start.9
  622.6 1.3 copy-start.10
  629.0 11.8 %copy-start.6 = (f32[1,288,32]{1,2,0:T(8,128)S(1)}, f32[1,288,32]{1,2,0:T(8,128)}, u32[]{:S(2)}) copy-start(f32[1,288,32]{1,2,0:T(8,128)} %param.14) | copy-start | bytes 110596
  629.6 11.2 %collective-permute-start.1 = (bf16[288,32]{0,1:T(8,128)(2,1)S(1)}, bf16[288,32]{0,1:T(8,128)(2,1)S(1)}, u32[]{:S(2)}, u32[]{:S(2)}) collective-permute-start(bf16[288,32]{0,1:T(8,128)(2,1)S(1)} %dynamic-slice_convert_fusion), channel_id=1, source_target_pairs={{0,128},{128,0},{1,129},{129,1},{2,130},{130,2},{3,131},{131,3},{4... | collective-permute-start | bytes 55304 | tf_op jit(solution)/shard_map/ppermute | solution.py:18
Sparse Core Ops, SparseCore 0:
  9.9 198.3 all-gather.2
  210.9 97.7 all-gather.4
where the time goes:
time: 649 us; the launch traced here: 648 us
  waiting for transfers between devices  522 us (80%)
  matrix products  47.4 us (7%)
  local copies, waits for them, and re-layouts  30.9 us (5%)
  other arithmetic  21.2 us (3%)
  between operations  15.5 us (2%)
  starting transfers between devices  11.2 us (2%)
    ppermute x7, waiting for transfers between devices, passed_along(): return lax.ppermute(value, axis, pairs)  247 us
    all_gather x1, waiting for transfers between devices, local(): qkv = add_rows(normed, lax.all_gather(w_qkv, 'req', axis=0, tiled=True))  198 us
    all_gather x1, waiting for transfers between devices, local(): lax.all_gather(w_out, 'req', axis=0, tiled=True)  75.5 us
    dot_general x8, matrix products, attend(): jnp.einsum('qhk,khd->qhd', probs.astype(jnp.bfloat16), values, preferred_...  26.5 us
    while x42, local copies, waits for them, and re-layouts  23.8 us
  transfers between devices with their start and end apart: 10, of which 9 were waited for; matrix products, arithmetic and copies ran while one was open for 4% of the time, Pallas kernels for 0%

commit v1 on v0

--- a/solution.py
+++ b/solution.py
@@ -85,7 +85,12 @@
     moved, result = lax.fori_loop(1, members, cycle_step, (stacked, first))
     top, total, weighted = result
     attended = (weighted / total[:, :, None]).reshape(rows, width).astype(jnp.bfloat16)
-    projected = add_rows(attended, lax.all_gather(w_out, "req", axis=0, tiled=True))
+    projected = add_rows(
+        attended,
+        jnp.concatenate(
+            lax.all_to_all(jnp.stack([w_out] * lax.axis_size("req")), "req", 0, 0), axis=0
+        ),
+    )
     block_out = (wide + modes[2] * projected).astype(jnp.bfloat16)
     head_in = (layer_norm(block_out.astype(jnp.float32)) * (1.0 + modes[4]) + modes[3]).astype(
         jnp.bfloat16

time: 649 us -> 679 us (1.046)
  waiting for transfers between devices: 522 us -> 539 us
  starting transfers between devices: 11.2 us -> 20.5 us
    all_gather x1, waiting for transfers between devices: 198 us -> 275 us  [local(): qkv = add_rows(normed, lax.all_gather(w_qkv, 'req', axis=0, tiled=True))]
    all_gather x1 -> x0, waiting for transfers between devices: 75.5 us -> none  [local(): lax.all_gather(w_out, 'req', axis=0, tiled=True)]
    ppermute x7, waiting for transfers between devices: 247 us -> 264 us  [passed_along(): return lax.ppermute(value, axis, pairs)]
    all_to_all x0 -> x1, starting transfers between devices: none -> 11.7 us  [local(): lax.all_to_all(jnp.stack([w_out] * lax.axis_size('req')), 'req', 0, 0)]
  transfers between devices with their start and end apart: 10 -> 10, of which waited for: 9 -> 8; matrix products, arithmetic and copies ran while one was open for 4% -> 4% of each run, Pallas kernels for 0% -> 0%
where the time goes in v1:
time: 679 us; the launch traced here: 678 us
  waiting for transfers between devices  539 us (79%)
  matrix products  47.3 us (7%)
  local copies, waits for them, and re-layouts  34.5 us (5%)
  starting transfers between devices  20.5 us (3%)
  other arithmetic  20.5 us (3%)
  between operations  15.5 us (2%)
    all_gather x1, waiting for transfers between devices, local(): qkv = add_rows(normed, lax.all_gather(w_qkv, 'req', axis=0, tiled=True))  275 us
    ppermute x7, waiting for transfers between devices, passed_along(): return lax.ppermute(value, axis, pairs)  264 us
    dot_general x8, matrix products, attend(): jnp.einsum('qhk,khd->qhd', probs.astype(jnp.bfloat16), values, preferred_...  26.4 us
    while x42, local copies, waits for them, and re-layouts  23.8 us
  transfers between devices with their start and end apart: 10, of which 8 were waited for; matrix products, arithmetic and copies ran while one was open for 4% of the time, Pallas kernels for 0%

profile of v1, /device:TPU:1, one launch (start us, length us, event | category | flops | bytes accessed | tf_op | source)
XLA Modules:
  0.0 678.2 jit_solution(9736170595470406454)
XLA Ops:
  7.3 3.6 stack.5
  10.8 11.7 %all-to-all-start = ((bf16[16,96,1536]{2,1,0:T(8,128)(2,1)}), bf16[16,96,1536]{2,1,0:T(8,128)(2,1)}, u32[]{:S(2)}, u32[]{:S(2)}) async-start(bf16[16,96,1536]{2,1,0:T(8,128)(2,1)} %stack.5), calls=%async_computation | async-start | bytes 9437184 | tf_op jit(solution)/shard_map/all_to_all | solution.py:91
  24.0 274.9 %all-gather.2.cloned.1.call-done = bf16[1536,4608]{1,0:T(8,128)(2,1)} async-done(((bf16[96,4608]{1,0:T(8,128)(2,1)}), bf16[1536,4608]{1,0:T(8,128)(2,1)}) %all-gather.2.cloned.1.call-update) | async-done | bytes 14155792 | tf_op jit(solution)/shard_map/all_gather | solution.py:65
  298.9 7.9 %fusion.42 = f32[288,4608]{1,0:T(8,128)S(1)} fusion(bf16[1536,4608]{1,0:T(8,128)(2,1)} %all-gather.2.cloned.1.call-done, bf16[1,1,288,1536]{3,2,1,0:T(8,128)(2,1)S(1)} %copy-done.2, f32[1536]{0:T(1024)S(1)} %get-tuple-element.226, f32[1536]{0:T(1024)S(1)} %get-tuple-element.227, f32[288]{0:T(512)S(1)} %add_sqrt_fusion.3, f32[288]{0:T(512)S(1)} %broadcast_multiply_fusion.1), kind=kOutput, calls=%fused_computation.61 | convolution fusion | flops 4079517696 | bytes 20363520 | tf_op jit(solution)/shard_map/dot_general | solution.py:31
  307.3 1.9 copy-done.1
  309.2 1.5 fusion.56
  310.7 1.0 copy-done.4
  313.4 1.7 copy.25
  315.3 1.0 copy-done.5
  316.3 1.0 bitcast_reduce_fusion.1
  317.2 1.5 fusion.21
  318.8 5.1 bitcast_add_fusion.1
  323.8 332.3 %while.21 = (s32[]{:T(128)}, bf16[2,288,12,128]{3,1,2,0:T(8,128)(2,1)}, f32[288,12]{0,1:T(8,128)S(1)}, f32[288,12]{0,1:T(8,128)S(1)}, f32[288,12,128]{2,0,1:T(8,...) while((s32[]{:T(128)}, ...), condition=%wide.region_9.10_spmd, body=%wide.region_6.9_spmd.sunk | while | flops 523439424 | bytes 44481960 | solution.py:85
  323.8 1.2 collective-permute-start
  325.7 39.2 %collective-permute-done = bf16[2,288,12,128]{3,1,2,0:T(8,128)(2,1)S(1)} collective-permute-done((bf16[2,288,12,128]{3,1,2,0:T(8,128)(2,1)}, bf16[2,288,12,128]{3,1,2,0:T(8,128)(2,1)S(1)}, u32[]{:S(2)}, u32[]{:S(2)}) %collective-permute-start) | collective-permute-done | bytes 1769504 | tf_op jit(solution)/shard_map/while/body/eval_jaxpr/ppermute | solution.py:12
  364.9 1.0 bitcast_reduce_fusion.3
  365.9 1.5 fusion.80
  367.4 1.3 copy.66
  368.7 0.8 copy-done.10
  369.5 3.0 bitcast_add_fusion.3
  372.6 1.3 copy-done.11
  374.5 39.6 %collective-permute-done = bf16[2,288,12,128]{3,1,2,0:T(8,128)(2,1)S(1)} collective-permute-done((bf16[2,288,12,128]{3,1,2,0:T(8,128)(2,1)}, bf16[2,288,12,128]{3,1,2,0:T(8,128)(2,1)S(1)}, u32[]{:S(2)}, u32[]{:S(2)}) %collective-permute-start) | collective-permute-done | bytes 1769504 | tf_op jit(solution)/shard_map/while/body/eval_jaxpr/ppermute | solution.py:12
  414.1 1.0 bitcast_reduce_fusion.3
  415.1 1.5 fusion.80
  416.6 1.3 copy.66
  417.8 0.8 copy-done.10
  418.7 3.0 bitcast_add_fusion.3
  421.8 1.3 copy-done.11
  423.7 38.7 %collective-permute-done = bf16[2,288,12,128]{3,1,2,0:T(8,128)(2,1)S(1)} collective-permute-done((bf16[2,288,12,128]{3,1,2,0:T(8,128)(2,1)}, bf16[2,288,12,128]{3,1,2,0:T(8,128)(2,1)S(1)}, u32[]{:S(2)}, u32[]{:S(2)}) %collective-permute-start) | collective-permute-done | bytes 1769504 | tf_op jit(solution)/shard_map/while/body/eval_jaxpr/ppermute | solution.py:12
  462.4 1.0 bitcast_reduce_fusion.3
  463.4 1.5 fusion.80
  464.9 1.3 copy.66
  466.2 0.8 copy-done.10
  467.0 3.0 bitcast_add_fusion.3
  470.1 1.3 copy-done.11
  472.0 37.9 %collective-permute-done = bf16[2,288,12,128]{3,1,2,0:T(8,128)(2,1)S(1)} collective-permute-done((bf16[2,288,12,128]{3,1,2,0:T(8,128)(2,1)}, bf16[2,288,12,128]{3,1,2,0:T(8,128)(2,1)S(1)}, u32[]{:S(2)}, u32[]{:S(2)}) %collective-permute-start) | collective-permute-done | bytes 1769504 | tf_op jit(solution)/shard_map/while/body/eval_jaxpr/ppermute | solution.py:12
  509.9 1.0 bitcast_reduce_fusion.3
  510.9 1.5 fusion.80
  512.4 1.3 copy.66
  513.6 0.8 copy-done.10
  514.5 3.0 bitcast_add_fusion.3
  517.6 1.3 copy-done.11
  519.5 37.0 %collective-permute-done = bf16[2,288,12,128]{3,1,2,0:T(8,128)(2,1)S(1)} collective-permute-done((bf16[2,288,12,128]{3,1,2,0:T(8,128)(2,1)}, bf16[2,288,12,128]{3,1,2,0:T(8,128)(2,1)S(1)}, u32[]{:S(2)}, u32[]{:S(2)}) %collective-permute-start) | collective-permute-done | bytes 1769504 | tf_op jit(solution)/shard_map/while/body/eval_jaxpr/ppermute | solution.py:12
  556.5 1.0 bitcast_reduce_fusion.3
  557.5 1.5 fusion.80
  559.0 1.3 copy.66
  560.2 0.8 copy-done.10
  561.1 3.0 bitcast_add_fusion.3
  564.2 1.3 copy-done.11
  566.1 36.1 %collective-permute-done = bf16[2,288,12,128]{3,1,2,0:T(8,128)(2,1)S(1)} collective-permute-done((bf16[2,288,12,128]{3,1,2,0:T(8,128)(2,1)}, bf16[2,288,12,128]{3,1,2,0:T(8,128)(2,1)S(1)}, u32[]{:S(2)}, u32[]{:S(2)}) %collective-permute-start) | collective-permute-done | bytes 1769504 | tf_op jit(solution)/shard_map/while/body/eval_jaxpr/ppermute | solution.py:12
  602.3 0.9 bitcast_reduce_fusion.3
  603.2 1.5 fusion.80
  604.7 1.3 copy.66
  606.0 0.8 copy-done.10
  606.8 3.0 bitcast_add_fusion.3
  609.9 1.3 copy-done.11
  611.9 35.3 %collective-permute-done = bf16[2,288,12,128]{3,1,2,0:T(8,128)(2,1)S(1)} collective-permute-done((bf16[2,288,12,128]{3,1,2,0:T(8,128)(2,1)}, bf16[2,288,12,128]{3,1,2,0:T(8,128)(2,1)S(1)}, u32[]{:S(2)}, u32[]{:S(2)}) %collective-permute-start) | collective-permute-done | bytes 1769504 | tf_op jit(solution)/shard_map/while/body/eval_jaxpr/ppermute | solution.py:12
  647.1 1.0 bitcast_reduce_fusion.3
  648.1 1.5 fusion.80
  649.6 1.3 copy.66
  651.7 3.0 bitcast_add_fusion.3
  654.8 1.3 copy-done.11
  656.1 4.8 fusion.67
  661.9 7.5 %collective-permute-start.1 = (bf16[288,32]{0,1:T(8,128)(2,1)S(1)}, bf16[288,32]{0,1:T(8,128)(2,1)S(1)}, u32[]{:S(2)}, u32[]{:S(2)}) collective-permute-start(bf16[288,32]{0,1:T(8,128)(2,1)S(1)} %dynamic-slice_convert_fusion), channel_id=1, source_target_pairs={{0,128},{128,0},{1,129},{129,1},{2,130},{130,2},{3,131},{131,3},{4... | collective-permute-start | bytes 55304 | tf_op jit(solution)/shard_map/ppermute | solution.py:18
  (91 shorter events, 10.9 us)
Async XLA Ops:
  6.5 654.7 %copy-start = (bf16[1536,64]{0,1:T(8,128)(2,1)S(1)}, bf16[1536,64]{0,1:T(8,128)(2,1)}, u32[]{:S(2)}) copy-start(bf16[1536,64]{0,1:T(8,128)(2,1)} %param.20) | copy-start | bytes 589828
  6.5 292.4 %all-gather.2.cloned.1.call-start = ((), (), s32[]{:S(2)}) async-start(), calls=%async_computation.1 | async-start | bytes 15040512 | tf_op jit(solution)/shard_map/all_gather | solution.py:65
  10.8 12.4 %copy-start.7 = (f32[1,5,1536]{2,0,1:T(1,128)S(1)}, f32[1,5,1536]{2,0,1:T(1,128)}, u32[]{:S(2)}) copy-start(f32[1,5,1536]{2,0,1:T(1,128)} %param.15) | copy-start | bytes 92164
  10.8 12.5 %copy-start.2 = (bf16[1,1,288,1536]{3,2,1,0:T(8,128)(2,1)S(1)}, bf16[1,1,288,1536]{3,2,1,0:T(8,128)(2,1)}, u32[]{:S(2)}) copy-start(bf16[1,1,288,1536]{3,2,1,0:T(8,128)(2,1)} %param.13) | copy-start | bytes 2654212
  10.8 313.0 %all-to-all-start = ((bf16[16,96,1536]{2,1,0:T(8,128)(2,1)}), bf16[16,96,1536]{2,1,0:T(8,128)(2,1)}, u32[]{:S(2)}, u32[]{:S(2)}) async-start(bf16[16,96,1536]{2,1,0:T(8,128)(2,1)} %stack.5), calls=%async_computation | async-start | bytes 9437184 | tf_op jit(solution)/shard_map/all_to_all | solution.py:91
  306.8 2.3 copy-start.1
  306.9 2.2 copy-start.8
  307.0 2.2 copy-start.9
  310.7 1.0 copy-start.4
  313.4 1.7 copy-start.3
  315.1 1.2 copy-start.5
  323.8 41.1 %collective-permute-start = (bf16[2,288,12,128]{3,1,2,0:T(8,128)(2,1)}, bf16[2,288,12,128]{3,1,2,0:T(8,128)(2,1)S(1)}, u32[]{:S(2)}, u32[]{:S(2)}) collective-permute-start(bf16[2,288,12,128]{3,1,2,0:T(8,128)(2,1)} %get-tuple-element.331), channel_id=1, source_target_pairs={{0,1},{1,2},{2,3},{3,4},{4,5},{5,6},{6,7},{7,0},{8,9},{9,10},{10,1... | collective-permute-start | bytes 5308424 | tf_op jit(solution)/shard_map/while/body/eval_jaxpr/ppermute | solution.py:12
  367.4 2.1 copy-start.10
  372.6 1.3 copy-start.11
  373.9 40.2 %collective-permute-start = (bf16[2,288,12,128]{3,1,2,0:T(8,128)(2,1)}, bf16[2,288,12,128]{3,1,2,0:T(8,128)(2,1)S(1)}, u32[]{:S(2)}, u32[]{:S(2)}) collective-permute-start(bf16[2,288,12,128]{3,1,2,0:T(8,128)(2,1)} %get-tuple-element.331), channel_id=1, source_target_pairs={{0,1},{1,2},{2,3},{3,4},{4,5},{5,6},{6,7},{7,0},{8,9},{9,10},{10,1... | collective-permute-start | bytes 5308424 | tf_op jit(solution)/shard_map/while/body/eval_jaxpr/ppermute | solution.py:12
  416.6 2.1 copy-start.10
  421.8 1.3 copy-start.11
  423.0 39.4 %collective-permute-start = (bf16[2,288,12,128]{3,1,2,0:T(8,128)(2,1)}, bf16[2,288,12,128]{3,1,2,0:T(8,128)(2,1)S(1)}, u32[]{:S(2)}, u32[]{:S(2)}) collective-permute-start(bf16[2,288,12,128]{3,1,2,0:T(8,128)(2,1)} %get-tuple-element.331), channel_id=1, source_target_pairs={{0,1},{1,2},{2,3},{3,4},{4,5},{5,6},{6,7},{7,0},{8,9},{9,10},{10,1... | collective-permute-start | bytes 5308424 | tf_op jit(solution)/shard_map/while/body/eval_jaxpr/ppermute | solution.py:12
  464.9 2.1 copy-start.10
  470.1 1.3 copy-start.11
  471.4 38.5 %collective-permute-start = (bf16[2,288,12,128]{3,1,2,0:T(8,128)(2,1)}, bf16[2,288,12,128]{3,1,2,0:T(8,128)(2,1)S(1)}, u32[]{:S(2)}, u32[]{:S(2)}) collective-permute-start(bf16[2,288,12,128]{3,1,2,0:T(8,128)(2,1)} %get-tuple-element.331), channel_id=1, source_target_pairs={{0,1},{1,2},{2,3},{3,4},{4,5},{5,6},{6,7},{7,0},{8,9},{9,10},{10,1... | collective-permute-start | bytes 5308424 | tf_op jit(solution)/shard_map/while/body/eval_jaxpr/ppermute | solution.py:12
  512.4 2.1 copy-start.10
  517.5 1.3 copy-start.11
  518.8 37.7 %collective-permute-start = (bf16[2,288,12,128]{3,1,2,0:T(8,128)(2,1)}, bf16[2,288,12,128]{3,1,2,0:T(8,128)(2,1)S(1)}, u32[]{:S(2)}, u32[]{:S(2)}) collective-permute-start(bf16[2,288,12,128]{3,1,2,0:T(8,128)(2,1)} %get-tuple-element.331), channel_id=1, source_target_pairs={{0,1},{1,2},{2,3},{3,4},{4,5},{5,6},{6,7},{7,0},{8,9},{9,10},{10,1... | collective-permute-start | bytes 5308424 | tf_op jit(solution)/shard_map/while/body/eval_jaxpr/ppermute | solution.py:12
  559.0 2.1 copy-start.10
  564.2 1.3 copy-start.11
  565.5 36.8 %collective-permute-start = (bf16[2,288,12,128]{3,1,2,0:T(8,128)(2,1)}, bf16[2,288,12,128]{3,1,2,0:T(8,128)(2,1)S(1)}, u32[]{:S(2)}, u32[]{:S(2)}) collective-permute-start(bf16[2,288,12,128]{3,1,2,0:T(8,128)(2,1)} %get-tuple-element.331), channel_id=1, source_target_pairs={{0,1},{1,2},{2,3},{3,4},{4,5},{5,6},{6,7},{7,0},{8,9},{9,10},{10,1... | collective-permute-start | bytes 5308424 | tf_op jit(solution)/shard_map/while/body/eval_jaxpr/ppermute | solution.py:12
  604.7 2.1 copy-start.10
  609.9 1.3 copy-start.11
  611.2 35.9 %collective-permute-start = (bf16[2,288,12,128]{3,1,2,0:T(8,128)(2,1)}, bf16[2,288,12,128]{3,1,2,0:T(8,128)(2,1)S(1)}, u32[]{:S(2)}, u32[]{:S(2)}) collective-permute-start(bf16[2,288,12,128]{3,1,2,0:T(8,128)(2,1)} %get-tuple-element.331), channel_id=1, source_target_pairs={{0,1},{1,2},{2,3},{3,4},{4,5},{5,6},{6,7},{7,0},{8,9},{9,10},{10,1... | collective-permute-start | bytes 5308424 | tf_op jit(solution)/shard_map/while/body/eval_jaxpr/ppermute | solution.py:12
  649.6 2.1 copy-start.10
  654.8 1.3 copy-start.11
  661.3 9.4 %copy-start.6 = (f32[1,288,32]{1,2,0:T(8,128)S(1)}, f32[1,288,32]{1,2,0:T(8,128)}, u32[]{:S(2)}) copy-start(f32[1,288,32]{1,2,0:T(8,128)} %param.14) | copy-start | bytes 110596
  661.9 8.8 %collective-permute-start.1 = (bf16[288,32]{0,1:T(8,128)(2,1)S(1)}, bf16[288,32]{0,1:T(8,128)(2,1)S(1)}, u32[]{:S(2)}, u32[]{:S(2)}) collective-permute-start(bf16[288,32]{0,1:T(8,128)(2,1)S(1)} %dynamic-slice_convert_fusion), channel_id=1, source_target_pairs={{0,128},{128,0},{1,129},{129,1},{2,130},{130,2},{3,131},{131,3},{4... | collective-permute-start | bytes 55304 | tf_op jit(solution)/shard_map/ppermute | solution.py:18
Sparse Core Ops, SparseCore 0:
  9.9 288.9 all-gather.1
